TPU v7x, 32 devices: a whole 2x2x4 slice. The times are simulated.
32 devices in a mesh: segment: 4 (over z), expert: 2 (over y), dp: 4 (over x, core).
Axes of the slice: x: 2, y: 2, z: 4, core: 2. Of those that a mesh axis runs over, the one named last changes fastest.
Arguments:
- state_in: bfloat16 [4, 4, 1024, 2048], P('segment', None, ('expert', 'dp')), may hold values from -6 to 6
- entering: bfloat16 [1, 4, 1024, 2048], P(None, None, ('expert', 'dp')), may hold values from -6 to 6
- saved: bfloat16 [4, 2, 2, 1024, 2048], P('segment', None, None, ('expert', 'dp')), may hold values from -6 to 6
- route_ids: int32 [4, 2, 4, 2, 1024, 6], P('segment', None, None, None, ('expert', 'dp')), may hold values from 0 to 63, as said below
- gate_vals: float32 [4, 2, 4, 2, 1024, 6], P('segment', None, None, None, ('expert', 'dp')), may hold values from 0.25 to 1
- w_gate: bfloat16 [4, 2, 2048, 1408], P('segment', 'expert', None, 'dp'), may hold values from -0.125 to 0.125
- w_up: bfloat16 [4, 2, 2048, 1408], P('segment', 'expert', None, 'dp'), may hold values from -0.125 to 0.125
- w_down: bfloat16 [4, 2, 1408, 2048], P('segment', 'expert', 'dp'), may hold values from -0.15625 to 0.15625
- gains: float32 [4, 2, 2048], P('segment'), may hold values from 0.5 to 2
Outputs:
- state_out: bfloat16 [4, 4, 1024, 2048], P('segment', None, ('expert', 'dp'))
Inputs may be any that keep to these rules, and one draw needn't show every extreme that they name: `route_ids`: the ids of one token are distinct, and a token names at most one id under 1. Within each block of 128 consecutive tokens (the tokens of one device) an id under 1 is named by at most 8 tokens. For every section, slot, unit and sublayer some id under 1 is named by exactly 8 tokens in every block, and every block has an id under 1 named by exactly 8 of its tokens.
All inputs are finite; a program needn't handle non-finite values.
Results may differ from a plain program's by a relative error of at most 0.017.
Values may be sent and summed in bfloat16 or wider, within the bound.
A program may use at most 128 MiB of HBM per device.

v0:
```python
import functools
import jax
import jax.numpy as jnp
from jax import lax
from jax.experimental import pallas as pl
from jax.experimental.pallas import tpu as pltpu
from jax.sharding import PartitionSpec as P

CAP = 8
EPSILON = 1e-06
LAST = (((1,), (1,)), ((), ()))
MESH = pl.DeviceIdType.MESH
BF = jnp.bfloat16
F32 = jnp.float32
ITEMS_OUT = (3, 4, 2, 2, 1)
ITEMS_BACK = (3, 2, 2, 2, 1)


def mm(a, b):
    return jnp.dot(a, b, preferred_element_type=F32)


def mm_t(a, b):
    return lax.dot_general(a, b, LAST, preferred_element_type=F32)


def mix(overlap, rows):
    return jnp.dot(overlap, rows, preferred_element_type=F32, precision=lax.Precision.HIGHEST)


def unit_norm(rows, gain):
    inv = lax.rsqrt(jnp.mean(rows * rows, axis=-1, keepdims=True) + EPSILON)
    return (rows * inv * gain).astype(BF), inv


def back_norm(rows, inv, gain, grad):
    weighted = gain * grad
    total = jnp.sum(weighted * rows, axis=-1, keepdims=True)
    return inv * weighted - rows * (inv * inv * inv) * total / rows.shape[-1]


def kernel(sizes, state, entering, saved, ids, gates, wg_in, wu_in, wd_in, gains, out, *scratch):
    ns, ne, nd = sizes
    group = ne * nd
    ec = ne // 2
    width = ec * CAP
    tokens, model = state.shape[1], state.shape[2]
    outs, ins, back_outs, back_ins = scratch[0:5], scratch[5:10], scratch[10:15], scratch[15:20]
    (base, patch_out, patch_in, sel, gate_col, vals, pre, wg, wu, wd,
     send_sem, recv_sem, local_sem, relay_send, relay_recv, enter_sem, weight_sem) = scratch[20:]
    seg, ex, dp = lax.axis_index("segment"), lax.axis_index("expert"), lax.axis_index("dp")
    me = ex * nd + dp

    weight_copies = [
        pltpu.make_async_copy(source, dest, weight_sem.at[i])
        for i, (source, dest) in enumerate(((wg_in, wg), (wu_in, wu), (wd_in, wd)))
    ]
    for copy in weight_copies:
        copy.start()

    barrier = pltpu.get_barrier_semaphore()

    @pl.loop(1, group)
    def _(k):
        t = lax.rem(me + k, group)
        pl.semaphore_signal(
            barrier, inc=1, device_id=(seg, lax.div(t, nd), lax.rem(t, nd)), device_id_type=MESH
        )

    has_up, has_down = seg < ns - 1, seg > 0

    @pl.when(has_up)
    def _():
        pl.semaphore_signal(barrier, inc=1, device_id=(seg + 1, ex, dp), device_id_type=MESH)

    @pl.when(has_down)
    def _():
        pl.semaphore_signal(barrier, inc=1, device_id=(seg - 1, ex, dp), device_id_type=MESH)

    neighbours = jnp.where(has_up, 1, 0) + jnp.where(has_down, 1, 0)
    pl.semaphore_wait(barrier, group - 1 + neighbours)

    def relay(unit, kind, source, dest):
        up = unit in (0, 3)
        goes, comes = (has_up, has_down) if up else (has_down, has_up)
        target = lax.rem(seg + (1 if up else ns - 1), ns)
        copy = pltpu.make_async_remote_copy(
            src_ref=source, dst_ref=dest, send_sem=relay_send.at[kind, unit],
            recv_sem=relay_recv.at[kind, unit], device_id=(target, ex, dp), device_id_type=MESH,
        )
        return goes, comes, copy

    def start_if(triple):
        @pl.when(triple[0])
        def _():
            triple[2].start()

    bulk = [relay(u, 0, state.at[u], base.at[u]) for u in range(4)]
    enter = [pltpu.make_async_copy(entering.at[u], base.at[u], enter_sem.at[u]) for u in range(4)]
    for u in range(4):
        start_if(bulk[u])

        @pl.when(jnp.logical_not(bulk[u][1]))
        def _(u=u):
            enter[u].start()

    def wait_bulk(u):
        @pl.when(bulk[u][1])
        def _():
            bulk[u][2].wait_recv()

        @pl.when(jnp.logical_not(bulk[u][1]))
        def _():
            enter[u].wait()

    patches = [relay(u, 1, patch_out.at[u], patch_in.at[u]) for u in range(4)]
    for u in range(4):
        @pl.when(jnp.logical_not(patches[u][1]))
        def _(u=u):
            patch_in[u] = jnp.zeros(patch_in.shape[1:], BF)

    def wait_patch(u):
        @pl.when(patches[u][1])
        def _():
            patches[u][2].wait_recv()

    def peer(t):
        return (seg, lax.div(t, nd), lax.rem(t, nd))

    def step_copy(r, k, outward, target):
        if outward:
            source, dest, phase = outs[r].at[lax.div(target, nd)], ins[r].at[me], 2 * r
        else:
            source, dest, phase = back_outs[r].at[target], back_ins[r].at[me], 2 * r + 1
        return pltpu.make_async_remote_copy(
            src_ref=source, dst_ref=dest, send_sem=send_sem.at[phase, k],
            recv_sem=recv_sem.at[phase, k], device_id=peer(target), device_id_type=MESH,
        )

    def own_copy(r, outward):
        if outward:
            return pltpu.make_async_copy(outs[r].at[ex], ins[r].at[me], local_sem.at[2 * r])
        return pltpu.make_async_copy(back_outs[r].at[me], back_ins[r].at[me], local_sem.at[2 * r + 1])

    def send(r, outward):
        @pl.loop(1, group)
        def _(k):
            step_copy(r, k, outward, lax.rem(me + k, group)).start()

        own_copy(r, outward).start()

    def receive(r, outward):
        phase = 2 * r if outward else 2 * r + 1
        arrived = ins[r] if outward else back_ins[r]

        @pl.loop(1, group)
        def _(k):
            slot = arrived.at[lax.rem(me - k + group, group)]
            pltpu.make_async_remote_copy(
                src_ref=slot, dst_ref=slot, send_sem=send_sem.at[phase, k],
                recv_sem=recv_sem.at[phase, k], device_id=peer(me), device_id_type=MESH,
            ).wait_recv()

        own_copy(r, outward).wait()

    def drain(r, outward):
        @pl.loop(1, group)
        def _(k):
            step_copy(r, k, outward, lax.rem(me + k, group)).wait_send()

    lane = lax.broadcasted_iota(jnp.int32, (tokens, tokens), 1)
    row = lax.broadcasted_iota(jnp.int32, (tokens, tokens), 0)
    before = (row < lane).astype(F32).astype(BF)
    eye = (row == lane).astype(F32)
    slot_row = lax.broadcasted_iota(jnp.int32, (CAP, tokens), 0).astype(F32)
    for e in range(ec):
        match = ids[...] == e
        routed = jnp.sum(match.astype(F32), axis=1)
        weight = jnp.sum(jnp.where(match, gates[...], 0.0), axis=1)
        earlier = mm(routed.astype(BF), before)
        for tb in range(ids.shape[0]):
            hit = (routed[tb:tb + 1] == 1.0) & (earlier[tb:tb + 1] == slot_row)
            one = jnp.where(hit, 1.0, 0.0)
            sel[tb, e * CAP:(e + 1) * CAP] = one
            gate_col[tb, e * CAP:(e + 1) * CAP] = jnp.broadcast_to(
                jnp.sum(one * weight[tb:tb + 1], axis=1, keepdims=True), (CAP, tokens)
            )

    def tab(slot, unit, sub):
        return (slot * 4 + unit) * 2 + sub

    def pick(slot, unit, values):
        first = unit % 2
        both = jnp.concatenate([sel[tab(slot, unit, first)], sel[tab(slot, unit, 1 - first)]])
        return mm(both.astype(BF), values)

    def pick_new(unit, old):
        first = unit % 2
        both = jnp.concatenate([sel[tab(1, unit, first)], sel[tab(1, unit, 1 - first)]])
        held = old[:, model:]
        keep = 1.0 - jnp.sum(held.astype(F32), axis=0, keepdims=True)
        moved = mm_t(both.astype(BF), held).astype(BF)
        return mm((both * keep).astype(BF), base[unit]) + mm(moved, old[:, :model])

    def overlap(slot, unit):
        first = unit % 2
        return mm_t(sel[tab(slot, unit, 1 - first)].astype(BF), sel[tab(slot, unit, first)].astype(BF))

    def overlap_t(slot, unit):
        first = unit % 2
        return mm_t(sel[tab(slot, unit, first)].astype(BF), sel[tab(slot, unit, 1 - first)].astype(BF))

    def gate(slot, unit, second):
        sub = 1 - unit % 2 if second else unit % 2
        return gate_col[tab(slot, unit, sub)][:, 0:1]

    def gain(unit, second):
        sub = 1 - unit % 2 if second else unit % 2
        return gains[sub:sub + 1]

    def put(r, item, unit, second, rows):
        side = 1 - unit % 2 if second else unit % 2
        for e in range(ec):
            outs[r][side * ec + e, item] = rows[e * CAP:(e + 1) * CAP].astype(BF)

    def got(r, item, unit, second):
        side = 1 - unit % 2 if second else unit % 2
        parts = []
        for e in range(ec):
            first = (side * ec + e) * nd
            total = back_ins[r][first, item].astype(F32)
            for q in range(1, nd):
                total = total + back_ins[r][first + q, item].astype(F32)
            parts.append(total)
        return parts[0] if ec == 1 else jnp.concatenate(parts)

    def rows_of(r, items):
        parts = [ins[r][:, i].astype(F32).reshape(group * CAP, model) for i in items]
        rows = parts[0] if len(parts) == 1 else jnp.concatenate(parts)
        return rows.astype(BF)

    def give(r, item, rows):
        back_outs[r][:, item] = rows.reshape(group, CAP, model).astype(BF)

    gr = group * CAP

    def half_forward(rows):
        return mm(rows, wg[...]), mm(rows, wu[...])

    def finish_forward(gp, up):
        return mm((gp * jax.nn.sigmoid(gp) * up).astype(BF), wd[...])

    def backward(rows, gp, up):
        act = mm_t(rows, wd[...])
        sig = jax.nn.sigmoid(gp)
        grad_gate = (act * up * sig * (1.0 + gp * (1.0 - sig))).astype(BF)
        grad_up = (act * gp * sig).astype(BF)
        return mm_t(grad_gate, wg[...]) + mm_t(grad_up, wu[...])

    names = ("fx1", "fx2", "k0a", "k0b", "k1a", "k1b", "d0a", "d0b", "d1a", "d1b", "g0", "g1")

    def at(name, st):
        return names.index(name) * 2 + st

    for st in range(2):
        f, b = st, 2 + st
        both = pick(0, f, state[f])
        vals[at("fx1", st)], vals[at("fx2", st)] = both[:width], both[width:]
        put(0, 0, f, False, unit_norm(both[:width], gain(f, False))[0])
        for slot in range(2):
            both = pick(slot, b, saved[slot, st])
            vals[at(f"k{slot}a", st)], vals[at(f"k{slot}b", st)] = both[:width], both[width:]
            put(0, 1 + slot, b, False, unit_norm(both[:width], gain(b, False))[0])
    send(0, True)
    for st in range(2):
        both = pick(0, 2 + st, state[2 + st])
        vals[at("d0a", st)], vals[at("d0b", st)] = both[:width], both[width:]
        put(1, 2, 2 + st, True, gate(0, 2 + st, True) * both[width:])
    for copy in weight_copies:
        copy.wait()
    receive(0, True)
    gp, up = half_forward(rows_of(0, (0, 1, 2)))
    for slot in range(2):
        pre[2 * slot] = gp[(1 + slot) * gr:(2 + slot) * gr]
        pre[2 * slot + 1] = up[(1 + slot) * gr:(2 + slot) * gr]
    rows = finish_forward(gp, up)
    for i in range(3):
        give(0, i, rows[i * gr:(i + 1) * gr])
    send(0, False)
    receive(0, False)

    def forward_middle(slot, st, r, item):
        add = gate(slot, st, False) * got(r, item, st, False)
        vals[at("fx1", st)] = vals[at("fx1", st)] + add
        middle = vals[at("fx2", st)] + mix(overlap(slot, st), add)
        vals[at("fx2", st)] = middle
        return unit_norm(middle, gain(st, True))[0]

    for st in range(2):
        put(1, 0, st, True, forward_middle(0, st, 0, 0))
        for slot in range(2):
            b = 2 + st
            add = gate(slot, b, False) * got(0, 1 + slot, b, False)
            middle = vals[at(f"k{slot}b", st)] + mix(overlap(slot, b), add)
            vals[at(f"k{slot}b", st)] = middle
            put(1, 1 if slot == 0 else 3, b, True, unit_norm(middle, gain(b, True))[0])
    send(1, True)
    receive(1, True)
    gp, up = half_forward(rows_of(1, (0, 1, 3)))
    pre[4], pre[5] = gp[2 * gr:], up[2 * gr:]
    give(1, 0, finish_forward(gp[:gr], up[:gr]))
    give(1, 1, backward(rows_of(1, (2,)), gp[gr:2 * gr], up[gr:2 * gr]))
    send(1, False)
    receive(1, False)

    def final_patch(slot, unit, first_rows, second_rows, last_second):
        a = unit % 2
        s1, s2 = sel[tab(slot, unit, a)], sel[tab(slot, unit, 1 - a)]
        if last_second:
            s1 = s1 * (1.0 - jnp.sum(s2, axis=0, keepdims=True))
        else:
            s2 = s2 * (1.0 - jnp.sum(s1, axis=0, keepdims=True))
        return (
            jnp.concatenate([first_rows, second_rows]).astype(BF),
            jnp.concatenate([s1, s2]).astype(BF),
        )

    def send_patch(unit, patch):
        patch_out[unit, :, :model] = patch[0]
        patch_out[unit, :, model:] = patch[1]
        start_if(patches[unit])

    def forward_end(slot, st, r, item):
        second = vals[at("fx2", st)] + gate(slot, st, True) * got(r, item, st, True)
        return final_patch(slot, st, vals[at("fx1", st)], second, True)

    def backward_middle(slot, st, r, item):
        b = 2 + st
        middle = vals[at(f"k{slot}b", st)]
        inv = unit_norm(middle, gain(b, True))[1]
        step = back_norm(middle, inv, gain(b, True), got(r, item, b, True))
        vals[at(f"d{slot}b", st)] = vals[at(f"d{slot}b", st)] + step
        inner = vals[at(f"d{slot}a", st)] + mix(overlap_t(slot, b), step)
        vals[at(f"d{slot}a", st)] = inner
        return gate(slot, b, False) * inner

    def backward_end(slot, st, r, item):
        b = 2 + st
        start = vals[at(f"k{slot}a", st)]
        inv = unit_norm(start, gain(b, False))[1]
        first = vals[at(f"d{slot}a", st)] + back_norm(start, inv, gain(b, False), got(r, item, b, False))
        return final_patch(slot, b, first, vals[at(f"d{slot}b", st)], False)

    for st in range(2):
        send_patch(st, forward_end(0, st, 1, 0))
    for st in range(2):
        put(2, 0, 2 + st, False, backward_middle(0, st, 1, 1))
    for st in range(2):
        wait_bulk(st)
        wait_patch(st)
        both = pick_new(st, patch_in[st])
        vals[at("fx1", st)], vals[at("fx2", st)] = both[:width], both[width:]
        put(2, 1, st, False, unit_norm(both[:width], gain(st, False))[0])
    send(2, True)
    receive(2, True)
    give(2, 0, backward(rows_of(2, (0,)), pre[0], pre[1]))
    gp, up = half_forward(rows_of(2, (1,)))
    give(2, 1, finish_forward(gp, up))
    send(2, False)
    receive(2, False)

    for st in range(2):
        send_patch(2 + st, backward_end(0, st, 2, 0))
    for st in range(2):
        put(3, 0, st, True, forward_middle(1, st, 2, 1))
    for st in range(2):
        u = 2 + st
        wait_bulk(u)
        wait_patch(u)
        both = pick_new(u, patch_in[u])
        vals[at("d1a", st)], vals[at("d1b", st)] = both[:width], both[width:]
        put(3, 1, u, True, gate(1, u, True) * both[width:])
    send(3, True)
    receive(3, True)
    gp, up = half_forward(rows_of(3, (0,)))
    give(3, 0, finish_forward(gp, up))
    give(3, 1, backward(rows_of(3, (1,)), pre[4], pre[5]))
    send(3, False)
    receive(3, False)

    def write(unit, patch):
        new_rows, new_sel = patch
        old = patch_in[unit]
        fresh = 1.0 - jnp.sum(new_sel.astype(F32), axis=0, keepdims=True)
        old_sel = old[:, model:].astype(F32) * fresh
        kept = eye * (fresh - jnp.sum(old_sel, axis=0, keepdims=True))
        spread = mm_t(eye.astype(BF), jnp.concatenate([old_sel.astype(BF), new_sel])).astype(BF)
        rows = jnp.concatenate([old[:, :model], new_rows])
        out[unit] = (mm(kept.astype(BF), base[unit]) + mm(spread, rows)).astype(BF)

    for st in range(2):
        put(4, 0, 2 + st, False, backward_middle(1, st, 3, 1))
    send(4, True)
    for st in range(2):
        write(st, forward_end(1, st, 3, 0))
    receive(4, True)
    give(4, 0, backward(rows_of(4, (0,)), pre[2], pre[3]))
    send(4, False)
    receive(4, False)
    for st in range(2):
        write(2 + st, backward_end(1, st, 4, 0))

    for r in range(5):
        drain(r, True)
        drain(r, False)
    for triple in bulk + patches:
        @pl.when(triple[0])
        def _(triple=triple):
            triple[2].wait_send()


def local(sizes, state_in, entering, saved, route_ids, gate_vals, w_gate, w_up, w_down, gains):
    ns, ne, nd = sizes
    group, width = ne * nd, ne // 2 * CAP
    units, tokens, model = state_in.shape[1:]
    hidden = w_gate.shape[-1]
    tables = route_ids.shape[1] * route_ids.shape[2] * route_ids.shape[3]
    topk = route_ids.shape[-1]
    ids = jnp.swapaxes(route_ids.reshape(tables, tokens, topk), 1, 2)
    gates = jnp.swapaxes(gate_vals.reshape(tables, tokens, topk), 1, 2)
    vmem = pl.BlockSpec(memory_space=pltpu.VMEM)
    anywhere = pl.BlockSpec(memory_space=pl.ANY)
    dma = pltpu.SemaphoreType.DMA
    scratch = (
        [pltpu.VMEM((ne, n, CAP, model), BF) for n in ITEMS_OUT]
        + [pltpu.VMEM((group, n, CAP, model), BF) for n in ITEMS_OUT]
        + [pltpu.VMEM((group, n, CAP, model), BF) for n in ITEMS_BACK]
        + [pltpu.VMEM((group, n, CAP, model), BF) for n in ITEMS_BACK]
        + [
            pltpu.VMEM((units, tokens, model), BF),
            pltpu.VMEM((units, 2 * width, model + tokens), BF),
            pltpu.VMEM((units, 2 * width, model + tokens), BF),
            pltpu.VMEM((tables, width, tokens), F32),
            pltpu.VMEM((tables, width, tokens), F32),
            pltpu.VMEM((24, width, model), F32),
            pltpu.VMEM((6, group * CAP, hidden), F32),
            pltpu.VMEM((model, hidden), BF),
            pltpu.VMEM((model, hidden), BF),
            pltpu.VMEM((hidden, model), BF),
            dma((10, group)), dma((10, group)), dma((10,)),
            dma((2, units)), dma((2, units)), dma((units,)), dma((3,)),
        ]
    )
    result = pl.pallas_call(
        functools.partial(kernel, sizes),
        out_shape=jax.ShapeDtypeStruct((units, tokens, model), BF),
        in_specs=[vmem, anywhere, vmem, vmem, vmem, anywhere, anywhere, anywhere, vmem],
        out_specs=vmem,
        scratch_shapes=scratch,
        compiler_params=pltpu.CompilerParams(
            collective_id=0, has_side_effects=True, vmem_limit_bytes=67043328
        ),
    )(state_in[0], entering[0], saved[0], ids, gates, w_gate[0, 0], w_up[0, 0], w_down[0, 0], gains[0])
    return result[None]


def solution(mesh):
    in_specs = (
        P("segment", None, ("expert", "dp"), None),
        P(None, None, ("expert", "dp"), None),
        P("segment", None, None, ("expert", "dp"), None),
        P("segment", None, None, None, ("expert", "dp"), None),
        P("segment", None, None, None, ("expert", "dp"), None),
        P("segment", "expert", None, "dp"),
        P("segment", "expert", None, "dp"),
        P("segment", "expert", "dp", None),
        P("segment", None, None),
    )
    out_specs = P("segment", None, ("expert", "dp"), None)
    sizes = (mesh.shape["segment"], mesh.shape["expert"], mesh.shape["dp"])
    body = functools.partial(local, sizes)
    return jax.shard_map(body, mesh=mesh, in_specs=in_specs, out_specs=out_specs, check_vma=False)
```

profile of v0, /device:TPU:0, one launch (start us, length us, event | category | flops | bytes accessed | tf_op | source)
XLA Modules:
  0.0 122.8 jit_solution(14201763610125612989)
XLA Ops:
  0.0 0.0 copy-start
  0.0 1.5 %copy.10 = s32[1,2,4,2,128,6]{4,5,3,2,1,0:T(8,128)} copy(s32[1,2,4,2,128,6]{4,3,5,2,1,0:T(2,128)} %param.12) | data formatting | bytes 98304 | tf_op args[3]
  1.5 1.4 %copy.11 = f32[1,2,4,2,128,6]{4,5,3,2,1,0:T(8,128)} copy(f32[1,2,4,2,128,6]{4,3,5,2,1,0:T(2,128)} %param.13) | data formatting | bytes 98304 | tf_op args[4]
  3.0 2.6 %copy.12 = bf16[1,1,2048,352]{3,2,1,0:T(8,128)(2,1)} copy(bf16[1,1,2048,352]{2,3,1,0:T(8,128)(2,1)} %param.14) | data formatting | bytes 2883584 | tf_op args[5]
  5.5 0.0 copy-done
  5.5 1.6 %copy.13 = bf16[1,1,2048,352]{3,2,1,0:T(8,128)(2,1)} copy(bf16[1,1,2048,352]{2,3,1,0:T(8,128)(2,1)S(1)} %copy-done) | data formatting | bytes 2883584 | tf_op args[6]
  7.1 112.6 %shard_map.91 = bf16[4,128,2048]{2,1,0:T(8,128)(2,1)} custom-call(bf16[4,128,2048]{2,1,0:T(8,128)(2,1)} %bitcast.17, bf16[4,128,2048]{2,1,0:T(8,128)(2,1)} %bitcast.18, bf16[2,2,128,2048]{3,2,1,0:T(8,128)(2,1)} %bitcast.19, s32[16,6,128]{2,1,0:T(8,128)} %bitcast.21, f32[16,6,128]{2,1,0:T(8,128)} %bitcast.22, bf16[2048,352]{1,0:T(8,128)(2,1)} %bitcast.15, ...), custom_call_target="tpu_custom_call" | custom-call | tf_op jit(solution)/shard_map/pallas_call | solution.py:454
  119.6 3.2 %copy.15 = bf16[1,4,128,2048]{3,2,1,0:T(8,128)(2,1)} copy(bf16[1,4,128,2048]{3,2,1,0:T(8,128)(2,1)} %bitcast.14) | data formatting | bytes 4194304
Async XLA Ops:
  0.0 5.5 %copy-start = (bf16[1,1,2048,352]{2,3,1,0:T(8,128)(2,1)S(1)}, bf16[1,1,2048,352]{2,3,1,0:T(8,128)(2,1)}, u32[]{:S(2)}) copy-start(bf16[1,1,2048,352]{2,3,1,0:T(8,128)(2,1)} %param.15) | copy-start | bytes 4325380
where the time goes:
time: 123 us
  Pallas kernels  113 us (92%)
  local copies, waits for them, and re-layouts  10.2 us (8%)
    pallas_call x1, Pallas kernels, local(): pl.pallas_call(functools.partial(kernel, sizes), out_shape=jax.ShapeDtype...  113 us
    unnamed x7, local copies, waits for them, and re-layouts  10.2 us

commit v1 on v0

--- a/solution.py
+++ b/solution.py
@@ -25,7 +25,12 @@
 
 
 def mix(overlap, rows):
-    return jnp.dot(overlap, rows, preferred_element_type=F32, precision=lax.Precision.HIGHEST)
+    picks = overlap.astype(BF)
+    high = rows.astype(BF)
+    rest = rows - high.astype(F32)
+    mid = rest.astype(BF)
+    low = (rest - mid.astype(F32)).astype(BF)
+    return mm(picks, high) + (mm(picks, mid) + mm(picks, low))
 
 
 def unit_norm(rows, gain):
@@ -39,18 +44,24 @@
     return inv * weighted - rows * (inv * inv * inv) * total / rows.shape[-1]
 
 
-def kernel(sizes, state, entering, saved, ids, gates, wg_in, wu_in, wd_in, gains, out, *scratch):
+def kernel(sizes, state_in, entering, saved_in, ids, gates, wg_in, wu_in, wd_in, gains, out, *scratch):
     ns, ne, nd = sizes
     group = ne * nd
     ec = ne // 2
     width = ec * CAP
-    tokens, model = state.shape[1], state.shape[2]
+    tokens, model = state_in.shape[1], state_in.shape[2]
     outs, ins, back_outs, back_ins = scratch[0:5], scratch[5:10], scratch[10:15], scratch[15:20]
     (base, patch_out, patch_in, sel, gate_col, vals, pre, wg, wu, wd,
-     send_sem, recv_sem, local_sem, relay_send, relay_recv, enter_sem, weight_sem) = scratch[20:]
+     send_sem, recv_sem, local_sem, relay_send, relay_recv, enter_sem, weight_sem, state, saved, input_sem) = scratch[20:]
     seg, ex, dp = lax.axis_index("segment"), lax.axis_index("expert"), lax.axis_index("dp")
     me = ex * nd + dp
 
+    input_copies = [
+        pltpu.make_async_copy(state_in, state, input_sem.at[0]),
+        pltpu.make_async_copy(saved_in, saved, input_sem.at[1]),
+    ]
+    for copy in input_copies:
+        copy.start()
     weight_copies = [
         pltpu.make_async_copy(source, dest, weight_sem.at[i])
         for i, (source, dest) in enumerate(((wg_in, wg), (wu_in, wu), (wd_in, wd)))
@@ -76,97 +87,6 @@
     @pl.when(has_down)
     def _():
         pl.semaphore_signal(barrier, inc=1, device_id=(seg - 1, ex, dp), device_id_type=MESH)
-
-    neighbours = jnp.where(has_up, 1, 0) + jnp.where(has_down, 1, 0)
-    pl.semaphore_wait(barrier, group - 1 + neighbours)
-
-    def relay(unit, kind, source, dest):
-        up = unit in (0, 3)
-        goes, comes = (has_up, has_down) if up else (has_down, has_up)
-        target = lax.rem(seg + (1 if up else ns - 1), ns)
-        copy = pltpu.make_async_remote_copy(
-            src_ref=source, dst_ref=dest, send_sem=relay_send.at[kind, unit],
-            recv_sem=relay_recv.at[kind, unit], device_id=(target, ex, dp), device_id_type=MESH,
-        )
-        return goes, comes, copy
-
-    def start_if(triple):
-        @pl.when(triple[0])
-        def _():
-            triple[2].start()
-
-    bulk = [relay(u, 0, state.at[u], base.at[u]) for u in range(4)]
-    enter = [pltpu.make_async_copy(entering.at[u], base.at[u], enter_sem.at[u]) for u in range(4)]
-    for u in range(4):
-        start_if(bulk[u])
-
-        @pl.when(jnp.logical_not(bulk[u][1]))
-        def _(u=u):
-            enter[u].start()
-
-    def wait_bulk(u):
-        @pl.when(bulk[u][1])
-        def _():
-            bulk[u][2].wait_recv()
-
-        @pl.when(jnp.logical_not(bulk[u][1]))
-        def _():
-            enter[u].wait()
-
-    patches = [relay(u, 1, patch_out.at[u], patch_in.at[u]) for u in range(4)]
-    for u in range(4):
-        @pl.when(jnp.logical_not(patches[u][1]))
-        def _(u=u):
-            patch_in[u] = jnp.zeros(patch_in.shape[1:], BF)
-
-    def wait_patch(u):
-        @pl.when(patches[u][1])
-        def _():
-            patches[u][2].wait_recv()
-
-    def peer(t):
-        return (seg, lax.div(t, nd), lax.rem(t, nd))
-
-    def step_copy(r, k, outward, target):
-        if outward:
-            source, dest, phase = outs[r].at[lax.div(target, nd)], ins[r].at[me], 2 * r
-        else:
-            source, dest, phase = back_outs[r].at[target], back_ins[r].at[me], 2 * r + 1
-        return pltpu.make_async_remote_copy(
-            src_ref=source, dst_ref=dest, send_sem=send_sem.at[phase, k],
-            recv_sem=recv_sem.at[phase, k], device_id=peer(target), device_id_type=MESH,
-        )
-
-    def own_copy(r, outward):
-        if outward:
-            return pltpu.make_async_copy(outs[r].at[ex], ins[r].at[me], local_sem.at[2 * r])
-        return pltpu.make_async_copy(back_outs[r].at[me], back_ins[r].at[me], local_sem.at[2 * r + 1])
-
-    def send(r, outward):
-        @pl.loop(1, group)
-        def _(k):
-            step_copy(r, k, outward, lax.rem(me + k, group)).start()
-
-        own_copy(r, outward).start()
-
-    def receive(r, outward):
-        phase = 2 * r if outward else 2 * r + 1
-        arrived = ins[r] if outward else back_ins[r]
-
-        @pl.loop(1, group)
-        def _(k):
-            slot = arrived.at[lax.rem(me - k + group, group)]
-            pltpu.make_async_remote_copy(
-                src_ref=slot, dst_ref=slot, send_sem=send_sem.at[phase, k],
-                recv_sem=recv_sem.at[phase, k], device_id=peer(me), device_id_type=MESH,
-            ).wait_recv()
-
-        own_copy(r, outward).wait()
-
-    def drain(r, outward):
-        @pl.loop(1, group)
-        def _(k):
-            step_copy(r, k, outward, lax.rem(me + k, group)).wait_send()
 
     lane = lax.broadcasted_iota(jnp.int32, (tokens, tokens), 1)
     row = lax.broadcasted_iota(jnp.int32, (tokens, tokens), 0)
@@ -186,6 +106,102 @@
                 jnp.sum(one * weight[tb:tb + 1], axis=1, keepdims=True), (CAP, tokens)
             )
 
+    neighbours = jnp.where(has_up, 1, 0) + jnp.where(has_down, 1, 0)
+    pl.semaphore_wait(barrier, group - 1 + neighbours)
+
+    def relay(unit, kind, source, dest):
+        up = unit in (0, 3)
+        goes, comes = (has_up, has_down) if up else (has_down, has_up)
+        target = lax.rem(seg + (1 if up else ns - 1), ns)
+        copy = pltpu.make_async_remote_copy(
+            src_ref=source, dst_ref=dest, send_sem=relay_send.at[kind, unit],
+            recv_sem=relay_recv.at[kind, unit], device_id=(target, ex, dp), device_id_type=MESH,
+        )
+        return goes, comes, copy
+
+    def start_if(triple):
+        @pl.when(triple[0])
+        def _():
+            triple[2].start()
+
+    bulk = [relay(u, 0, state_in.at[u], base.at[u]) for u in range(4)]
+    enter = [pltpu.make_async_copy(entering.at[u], base.at[u], enter_sem.at[u]) for u in range(4)]
+    for u in range(4):
+        start_if(bulk[u])
+
+        @pl.when(jnp.logical_not(bulk[u][1]))
+        def _(u=u):
+            enter[u].start()
+
+    def wait_bulk(u):
+        @pl.when(bulk[u][1])
+        def _():
+            bulk[u][2].wait_recv()
+
+        @pl.when(jnp.logical_not(bulk[u][1]))
+        def _():
+            enter[u].wait()
+
+    patches = [relay(u, 1, patch_out.at[u], patch_in.at[u]) for u in range(4)]
+    for u in range(4):
+        @pl.when(jnp.logical_not(patches[u][1]))
+        def _(u=u):
+            patch_in[u] = jnp.zeros(patch_in.shape[1:], BF)
+
+    def wait_patch(u):
+        @pl.when(patches[u][1])
+        def _():
+            patches[u][2].wait_recv()
+
+    def peer(t):
+        return (seg, lax.div(t, nd), lax.rem(t, nd))
+
+    def phase_of(r, outward, item):
+        return sum(ITEMS_OUT[:r]) + item if outward else sum(ITEMS_OUT) + sum(ITEMS_BACK[:r]) + item
+
+    def step_copy(r, k, outward, item, target):
+        if outward:
+            source, dest = outs[r].at[lax.div(target, nd), item], ins[r].at[me, item]
+        else:
+            source, dest = back_outs[r].at[target, item], back_ins[r].at[me, item]
+        phase = phase_of(r, outward, item)
+        return pltpu.make_async_remote_copy(
+            src_ref=source, dst_ref=dest, send_sem=send_sem.at[phase, k],
+            recv_sem=recv_sem.at[phase, k], device_id=peer(target), device_id_type=MESH,
+        )
+
+    def own_copy(r, outward, item):
+        source = outs[r].at[ex, item] if outward else back_outs[r].at[me, item]
+        dest = ins[r].at[me, item] if outward else back_ins[r].at[me, item]
+        return pltpu.make_async_copy(source, dest, local_sem.at[phase_of(r, outward, item)])
+
+    def send(r, outward, item):
+        @pl.loop(1, group)
+        def _(k):
+            step_copy(r, k, outward, item, lax.rem(me + k, group)).start()
+
+        own_copy(r, outward, item).start()
+
+    def receive(r, outward, *items):
+        arrived = ins[r] if outward else back_ins[r]
+        for item in items:
+            phase = phase_of(r, outward, item)
+
+            @pl.loop(1, group)
+            def _(k, item=item, phase=phase):
+                slot = arrived.at[lax.rem(me - k + group, group), item]
+                pltpu.make_async_remote_copy(
+                    src_ref=slot, dst_ref=slot, send_sem=send_sem.at[phase, k],
+                    recv_sem=recv_sem.at[phase, k], device_id=peer(me), device_id_type=MESH,
+                ).wait_recv()
+
+            own_copy(r, outward, item).wait()
+
+    def drain(r, outward, item):
+        @pl.loop(1, group)
+        def _(k):
+            step_copy(r, k, outward, item, lax.rem(me + k, group)).wait_send()
+
     def tab(slot, unit, sub):
         return (slot * 4 + unit) * 2 + sub
 
@@ -262,56 +278,12 @@
     def at(name, st):
         return names.index(name) * 2 + st
 
-    for st in range(2):
-        f, b = st, 2 + st
-        both = pick(0, f, state[f])
-        vals[at("fx1", st)], vals[at("fx2", st)] = both[:width], both[width:]
-        put(0, 0, f, False, unit_norm(both[:width], gain(f, False))[0])
-        for slot in range(2):
-            both = pick(slot, b, saved[slot, st])
-            vals[at(f"k{slot}a", st)], vals[at(f"k{slot}b", st)] = both[:width], both[width:]
-            put(0, 1 + slot, b, False, unit_norm(both[:width], gain(b, False))[0])
-    send(0, True)
-    for st in range(2):
-        both = pick(0, 2 + st, state[2 + st])
-        vals[at("d0a", st)], vals[at("d0b", st)] = both[:width], both[width:]
-        put(1, 2, 2 + st, True, gate(0, 2 + st, True) * both[width:])
-    for copy in weight_copies:
-        copy.wait()
-    receive(0, True)
-    gp, up = half_forward(rows_of(0, (0, 1, 2)))
-    for slot in range(2):
-        pre[2 * slot] = gp[(1 + slot) * gr:(2 + slot) * gr]
-        pre[2 * slot + 1] = up[(1 + slot) * gr:(2 + slot) * gr]
-    rows = finish_forward(gp, up)
-    for i in range(3):
-        give(0, i, rows[i * gr:(i + 1) * gr])
-    send(0, False)
-    receive(0, False)
-
     def forward_middle(slot, st, r, item):
         add = gate(slot, st, False) * got(r, item, st, False)
         vals[at("fx1", st)] = vals[at("fx1", st)] + add
         middle = vals[at("fx2", st)] + mix(overlap(slot, st), add)
         vals[at("fx2", st)] = middle
         return unit_norm(middle, gain(st, True))[0]
-
-    for st in range(2):
-        put(1, 0, st, True, forward_middle(0, st, 0, 0))
-        for slot in range(2):
-            b = 2 + st
-            add = gate(slot, b, False) * got(0, 1 + slot, b, False)
-            middle = vals[at(f"k{slot}b", st)] + mix(overlap(slot, b), add)
-            vals[at(f"k{slot}b", st)] = middle
-            put(1, 1 if slot == 0 else 3, b, True, unit_norm(middle, gain(b, True))[0])
-    send(1, True)
-    receive(1, True)
-    gp, up = half_forward(rows_of(1, (0, 1, 3)))
-    pre[4], pre[5] = gp[2 * gr:], up[2 * gr:]
-    give(1, 0, finish_forward(gp[:gr], up[:gr]))
-    give(1, 1, backward(rows_of(1, (2,)), gp[gr:2 * gr], up[gr:2 * gr]))
-    send(1, False)
-    receive(1, False)
 
     def final_patch(slot, unit, first_rows, second_rows, last_second):
         a = unit % 2
@@ -351,43 +323,6 @@
         first = vals[at(f"d{slot}a", st)] + back_norm(start, inv, gain(b, False), got(r, item, b, False))
         return final_patch(slot, b, first, vals[at(f"d{slot}b", st)], False)
 
-    for st in range(2):
-        send_patch(st, forward_end(0, st, 1, 0))
-    for st in range(2):
-        put(2, 0, 2 + st, False, backward_middle(0, st, 1, 1))
-    for st in range(2):
-        wait_bulk(st)
-        wait_patch(st)
-        both = pick_new(st, patch_in[st])
-        vals[at("fx1", st)], vals[at("fx2", st)] = both[:width], both[width:]
-        put(2, 1, st, False, unit_norm(both[:width], gain(st, False))[0])
-    send(2, True)
-    receive(2, True)
-    give(2, 0, backward(rows_of(2, (0,)), pre[0], pre[1]))
-    gp, up = half_forward(rows_of(2, (1,)))
-    give(2, 1, finish_forward(gp, up))
-    send(2, False)
-    receive(2, False)
-
-    for st in range(2):
-        send_patch(2 + st, backward_end(0, st, 2, 0))
-    for st in range(2):
-        put(3, 0, st, True, forward_middle(1, st, 2, 1))
-    for st in range(2):
-        u = 2 + st
-        wait_bulk(u)
-        wait_patch(u)
-        both = pick_new(u, patch_in[u])
-        vals[at("d1a", st)], vals[at("d1b", st)] = both[:width], both[width:]
-        put(3, 1, u, True, gate(1, u, True) * both[width:])
-    send(3, True)
-    receive(3, True)
-    gp, up = half_forward(rows_of(3, (0,)))
-    give(3, 0, finish_forward(gp, up))
-    give(3, 1, backward(rows_of(3, (1,)), pre[4], pre[5]))
-    send(3, False)
-    receive(3, False)
-
     def write(unit, patch):
         new_rows, new_sel = patch
         old = patch_in[unit]
@@ -398,21 +333,134 @@
         rows = jnp.concatenate([old[:, :model], new_rows])
         out[unit] = (mm(kept.astype(BF), base[unit]) + mm(spread, rows)).astype(BF)
 
-    for st in range(2):
+    both_streams = range(2)
+
+    def start_kept(slot, item):
+        for st in both_streams:
+            b = 2 + st
+            both = pick(slot, b, saved[slot, st])
+            vals[at(f"k{slot}a", st)], vals[at(f"k{slot}b", st)] = both[:width], both[width:]
+            put(0, item, b, False, unit_norm(both[:width], gain(b, False))[0])
+        send(0, True, item)
+
+    def middle_kept(slot, item, to):
+        receive(0, False, item)
+        for st in both_streams:
+            b = 2 + st
+            add = gate(slot, b, False) * got(0, item, b, False)
+            middle = vals[at(f"k{slot}b", st)] + mix(overlap(slot, b), add)
+            vals[at(f"k{slot}b", st)] = middle
+            put(1, to, b, True, unit_norm(middle, gain(b, True))[0])
+        send(1, True, to)
+
+    input_copies[0].wait()
+    for st in both_streams:
+        both = pick(0, st, state[st])
+        vals[at("fx1", st)], vals[at("fx2", st)] = both[:width], both[width:]
+        put(0, 0, st, False, unit_norm(both[:width], gain(st, False))[0])
+    send(0, True, 0)
+    input_copies[1].wait()
+    start_kept(0, 1)
+    for st in both_streams:
+        both = pick(0, 2 + st, state[2 + st])
+        vals[at("d0a", st)], vals[at("d0b", st)] = both[:width], both[width:]
+        put(1, 2, 2 + st, True, gate(0, 2 + st, True) * both[width:])
+    send(1, True, 2)
+    for copy in weight_copies:
+        copy.wait()
+    receive(0, True, 0)
+    gp, up = half_forward(rows_of(0, (0,)))
+    give(0, 0, finish_forward(gp, up))
+    send(0, False, 0)
+    receive(0, True, 1)
+    gp, up = half_forward(rows_of(0, (1,)))
+    pre[0], pre[1] = gp, up
+    give(0, 1, finish_forward(gp, up))
+    send(0, False, 1)
+    start_kept(1, 2)
+    receive(0, False, 0)
+    for st in both_streams:
+        put(1, 0, st, True, forward_middle(0, st, 0, 0))
+    send(1, True, 0)
+    middle_kept(0, 1, 1)
+    receive(0, True, 2)
+    gp, up = half_forward(rows_of(0, (2,)))
+    pre[2], pre[3] = gp, up
+    give(0, 2, finish_forward(gp, up))
+    send(0, False, 2)
+
+    receive(1, True, 0)
+    give(1, 0, finish_forward(*half_forward(rows_of(1, (0,)))))
+    send(1, False, 0)
+    receive(1, True, 1, 2)
+    gp, up = half_forward(rows_of(1, (1,)))
+    give(1, 1, backward(rows_of(1, (2,)), gp, up))
+    send(1, False, 1)
+    receive(1, False, 0)
+    for st in both_streams:
+        send_patch(st, forward_end(0, st, 1, 0))
+    middle_kept(1, 2, 3)
+    receive(1, False, 1)
+    for st in both_streams:
+        put(2, 0, 2 + st, False, backward_middle(0, st, 1, 1))
+    send(2, True, 0)
+
+    for st in both_streams:
+        wait_bulk(st)
+        wait_patch(st)
+        both = pick_new(st, patch_in[st])
+        vals[at("fx1", st)], vals[at("fx2", st)] = both[:width], both[width:]
+        put(2, 1, st, False, unit_norm(both[:width], gain(st, False))[0])
+    send(2, True, 1)
+    receive(2, True, 0)
+    give(2, 0, backward(rows_of(2, (0,)), pre[0], pre[1]))
+    send(2, False, 0)
+    receive(2, True, 1)
+    give(2, 1, finish_forward(*half_forward(rows_of(2, (1,)))))
+    send(2, False, 1)
+    receive(1, True, 3)
+    pre[4], pre[5] = half_forward(rows_of(1, (3,)))
+    receive(2, False, 0)
+    for st in both_streams:
+        send_patch(2 + st, backward_end(0, st, 2, 0))
+    receive(2, False, 1)
+    for st in both_streams:
+        put(3, 0, st, True, forward_middle(1, st, 2, 1))
+
+    for st in both_streams:
+        u = 2 + st
+        wait_bulk(u)
+        wait_patch(u)
+        both = pick_new(u, patch_in[u])
+        vals[at("d1a", st)], vals[at("d1b", st)] = both[:width], both[width:]
+        put(3, 1, u, True, gate(1, u, True) * both[width:])
+    send(3, True, 1)
+    send(3, True, 0)
+    receive(3, True, 1)
+    give(3, 1, backward(rows_of(3, (1,)), pre[4], pre[5]))
+    send(3, False, 1)
+    receive(3, True, 0)
+    give(3, 0, finish_forward(*half_forward(rows_of(3, (0,)))))
+    send(3, False, 0)
+    receive(3, False, 1)
+    for st in both_streams:
         put(4, 0, 2 + st, False, backward_middle(1, st, 3, 1))
-    send(4, True)
-    for st in range(2):
+    send(4, True, 0)
+    receive(3, False, 0)
+    for st in both_streams:
         write(st, forward_end(1, st, 3, 0))
-    receive(4, True)
+    receive(4, True, 0)
     give(4, 0, backward(rows_of(4, (0,)), pre[2], pre[3]))
-    send(4, False)
-    receive(4, False)
-    for st in range(2):
+    send(4, False, 0)
+    receive(4, False, 0)
+    for st in both_streams:
         write(2 + st, backward_end(1, st, 4, 0))
 
     for r in range(5):
-        drain(r, True)
-        drain(r, False)
+        for item in range(ITEMS_OUT[r]):
+            drain(r, True, item)
+        for item in range(ITEMS_BACK[r]):
+            drain(r, False, item)
     for triple in bulk + patches:
         @pl.when(triple[0])
         def _(triple=triple):
@@ -447,14 +495,17 @@
             pltpu.VMEM((model, hidden), BF),
             pltpu.VMEM((model, hidden), BF),
             pltpu.VMEM((hidden, model), BF),
-            dma((10, group)), dma((10, group)), dma((10,)),
+            dma((22, group)), dma((22, group)), dma((22,)),
             dma((2, units)), dma((2, units)), dma((units,)), dma((3,)),
+            pltpu.VMEM((units, tokens, model), BF),
+            pltpu.VMEM(saved.shape[1:], BF),
+            dma((2,)),
         ]
     )
     result = pl.pallas_call(
         functools.partial(kernel, sizes),
         out_shape=jax.ShapeDtypeStruct((units, tokens, model), BF),
-        in_specs=[vmem, anywhere, vmem, vmem, vmem, anywhere, anywhere, anywhere, vmem],
+        in_specs=[anywhere, anywhere, anywhere, vmem, vmem, anywhere, anywhere, anywhere, vmem],
         out_specs=vmem,
         scratch_shapes=scratch,
         compiler_params=pltpu.CompilerParams(

time: 123 us -> 98.4 us (0.80)
  Pallas kernels: 113 us -> 87.9 us
    pallas_call x1, Pallas kernels: 113 us -> 87.9 us  [local(): pl.pallas_call(functools.partial(kernel, sizes), out_shape=jax.ShapeDtype...]
where the time goes in v1:
time: 98.4 us; the launch traced here: 98.1 us
  Pallas kernels  87.9 us (89%)
  local copies, waits for them, and re-layouts  10.2 us (10%)
    pallas_call x1, Pallas kernels, local(): pl.pallas_call(functools.partial(kernel, sizes), out_shape=jax.ShapeDtype...  87.9 us
    unnamed x7, local copies, waits for them, and re-layouts  10.2 us

profile of v1, /device:TPU:0, one launch (start us, length us, event | category | flops | bytes accessed | tf_op | source)
XLA Modules:
  0.0 98.1 jit_solution(15546228920081003953)
XLA Ops:
  0.0 0.0 copy-start
  0.0 1.5 %copy.10 = s32[1,2,4,2,128,6]{4,5,3,2,1,0:T(8,128)} copy(s32[1,2,4,2,128,6]{4,3,5,2,1,0:T(2,128)} %param.12) | data formatting | bytes 98304 | tf_op args[3]
  1.5 1.4 %copy.11 = f32[1,2,4,2,128,6]{4,5,3,2,1,0:T(8,128)} copy(f32[1,2,4,2,128,6]{4,3,5,2,1,0:T(2,128)} %param.13) | data formatting | bytes 98304 | tf_op args[4]
  3.0 2.6 %copy.12 = bf16[1,1,2048,352]{3,2,1,0:T(8,128)(2,1)} copy(bf16[1,1,2048,352]{2,3,1,0:T(8,128)(2,1)} %param.14) | data formatting | bytes 2883584 | tf_op args[5]
  5.5 0.0 copy-done
  5.5 1.6 %copy.13 = bf16[1,1,2048,352]{3,2,1,0:T(8,128)(2,1)} copy(bf16[1,1,2048,352]{2,3,1,0:T(8,128)(2,1)S(1)} %copy-done) | data formatting | bytes 2883584 | tf_op args[6]
  7.1 87.9 %shard_map.91 = bf16[4,128,2048]{2,1,0:T(8,128)(2,1)} custom-call(bf16[4,128,2048]{2,1,0:T(8,128)(2,1)} %bitcast.17, bf16[4,128,2048]{2,1,0:T(8,128)(2,1)} %bitcast.18, bf16[2,2,128,2048]{3,2,1,0:T(8,128)(2,1)} %bitcast.19, s32[16,6,128]{2,1,0:T(8,128)} %bitcast.21, f32[16,6,128]{2,1,0:T(8,128)} %bitcast.22, bf16[2048,352]{1,0:T(8,128)(2,1)} %bitcast.15, ...), custom_call_target="tpu_custom_call" | custom-call | tf_op jit(solution)/shard_map/pallas_call | solution.py:505
  95.0 3.2 %copy.15 = bf16[1,4,128,2048]{3,2,1,0:T(8,128)(2,1)} copy(bf16[1,4,128,2048]{3,2,1,0:T(8,128)(2,1)} %bitcast.14) | data formatting | bytes 4194304
Async XLA Ops:
  0.0 5.5 %copy-start = (bf16[1,1,2048,352]{2,3,1,0:T(8,128)(2,1)S(1)}, bf16[1,1,2048,352]{2,3,1,0:T(8,128)(2,1)}, u32[]{:S(2)}) copy-start(bf16[1,1,2048,352]{2,3,1,0:T(8,128)(2,1)} %param.15) | copy-start | bytes 4325380

commit v2 on v1

--- a/solution.py
+++ b/solution.py
@@ -377,17 +377,12 @@
     pre[0], pre[1] = gp, up
     give(0, 1, finish_forward(gp, up))
     send(0, False, 1)
-    start_kept(1, 2)
     receive(0, False, 0)
     for st in both_streams:
         put(1, 0, st, True, forward_middle(0, st, 0, 0))
     send(1, True, 0)
     middle_kept(0, 1, 1)
-    receive(0, True, 2)
-    gp, up = half_forward(rows_of(0, (2,)))
-    pre[2], pre[3] = gp, up
-    give(0, 2, finish_forward(gp, up))
-    send(0, False, 2)
+    start_kept(1, 2)
 
     receive(1, True, 0)
     give(1, 0, finish_forward(*half_forward(rows_of(1, (0,)))))
@@ -396,10 +391,14 @@
     gp, up = half_forward(rows_of(1, (1,)))
     give(1, 1, backward(rows_of(1, (2,)), gp, up))
     send(1, False, 1)
+    receive(0, True, 2)
+    gp, up = half_forward(rows_of(0, (2,)))
+    pre[2], pre[3] = gp, up
+    give(0, 2, finish_forward(gp, up))
+    send(0, False, 2)
     receive(1, False, 0)
     for st in both_streams:
         send_patch(st, forward_end(0, st, 1, 0))
-    middle_kept(1, 2, 3)
     receive(1, False, 1)
     for st in both_streams:
         put(2, 0, 2 + st, False, backward_middle(0, st, 1, 1))
@@ -412,6 +411,7 @@
         vals[at("fx1", st)], vals[at("fx2", st)] = both[:width], both[width:]
         put(2, 1, st, False, unit_norm(both[:width], gain(st, False))[0])
     send(2, True, 1)
+    middle_kept(1, 2, 3)
     receive(2, True, 0)
     give(2, 0, backward(rows_of(2, (0,)), pre[0], pre[1]))
     send(2, False, 0)

time: 98.4 us -> 96.8 us (0.984)
  Pallas kernels: 87.9 us -> 86.3 us
    pallas_call x1, Pallas kernels: 87.9 us -> 86.3 us  [local(): pl.pallas_call(functools.partial(kernel, sizes), out_shape=jax.ShapeDtype...]
where the time goes in v2:
time: 96.8 us; the launch traced here: 96.6 us
  Pallas kernels  86.3 us (89%)
  local copies, waits for them, and re-layouts  10.2 us (11%)
    pallas_call x1, Pallas kernels, local(): pl.pallas_call(functools.partial(kernel, sizes), out_shape=jax.ShapeDtype...  86.3 us
    unnamed x7, local copies, waits for them, and re-layouts  10.2 us

profile of v2, /device:TPU:0, one launch (start us, length us, event | category | flops | bytes accessed | tf_op | source)
XLA Modules:
  0.0 96.6 jit_solution(12688548829945891079)
XLA Ops:
  0.0 0.0 copy-start
  0.0 1.5 %copy.10 = s32[1,2,4,2,128,6]{4,5,3,2,1,0:T(8,128)} copy(s32[1,2,4,2,128,6]{4,3,5,2,1,0:T(2,128)} %param.12) | data formatting | bytes 98304 | tf_op args[3]
  1.5 1.4 %copy.11 = f32[1,2,4,2,128,6]{4,5,3,2,1,0:T(8,128)} copy(f32[1,2,4,2,128,6]{4,3,5,2,1,0:T(2,128)} %param.13) | data formatting | bytes 98304 | tf_op args[4]
  3.0 2.6 %copy.12 = bf16[1,1,2048,352]{3,2,1,0:T(8,128)(2,1)} copy(bf16[1,1,2048,352]{2,3,1,0:T(8,128)(2,1)} %param.14) | data formatting | bytes 2883584 | tf_op args[5]
  5.5 0.0 copy-done
  5.5 1.6 %copy.13 = bf16[1,1,2048,352]{3,2,1,0:T(8,128)(2,1)} copy(bf16[1,1,2048,352]{2,3,1,0:T(8,128)(2,1)S(1)} %copy-done) | data formatting | bytes 2883584 | tf_op args[6]
  7.1 86.3 %shard_map.91 = bf16[4,128,2048]{2,1,0:T(8,128)(2,1)} custom-call(bf16[4,128,2048]{2,1,0:T(8,128)(2,1)} %bitcast.17, bf16[4,128,2048]{2,1,0:T(8,128)(2,1)} %bitcast.18, bf16[2,2,128,2048]{3,2,1,0:T(8,128)(2,1)} %bitcast.19, s32[16,6,128]{2,1,0:T(8,128)} %bitcast.21, f32[16,6,128]{2,1,0:T(8,128)} %bitcast.22, bf16[2048,352]{1,0:T(8,128)(2,1)} %bitcast.15, ...), custom_call_target="tpu_custom_call" | custom-call | tf_op jit(solution)/shard_map/pallas_call | solution.py:505
  93.4 3.2 %copy.15 = bf16[1,4,128,2048]{3,2,1,0:T(8,128)(2,1)} copy(bf16[1,4,128,2048]{3,2,1,0:T(8,128)(2,1)} %bitcast.14) | data formatting | bytes 4194304
Async XLA Ops:
  0.0 5.5 %copy-start = (bf16[1,1,2048,352]{2,3,1,0:T(8,128)(2,1)S(1)}, bf16[1,1,2048,352]{2,3,1,0:T(8,128)(2,1)}, u32[]{:S(2)}) copy-start(bf16[1,1,2048,352]{2,3,1,0:T(8,128)(2,1)} %param.15) | copy-start | bytes 4325380
